TPU v7x, 256 devices: a whole 4x4x8 slice. The times are simulated.
256 devices in a mesh: dp: 32 (over z, y), tensor: 8 (over x, core).
Axes of the slice: x: 4, y: 4, z: 8, core: 2. Of those that a mesh axis runs over, the one named last changes fastest.
Arguments:
- hidden: bfloat16 [4096, 26624], P('dp', 'tensor'), may hold values from -6 to 6
- out_grad: bfloat16 [4096, 8192], P(('dp', 'tensor')), may hold values from -0.375 to 0.375
- master: float32 [8192, 26624], P('dp', 'tensor'), may hold values from -0.3125 to 0.3125
- first_moment: bfloat16 [8192, 26624], P('dp', 'tensor'), may hold values from -4 to 4
- second_moment: bfloat16 [8192, 26624], P('dp', 'tensor'), may hold values from 0.049804688 to 1
- row_counts: int32 [8], replicated, may hold values from 2816 to 3840, as said below
- step_count: int32 [1], replicated, may hold values from 1 to 11
Outputs:
- adam_update: float32 [8192, 26624], P('dp', 'tensor')
- weights_tp: bfloat16 [8192, 30720], P('dp', 'tensor')
Inputs may be any that keep to these rules, and one draw needn't show every extreme that they name: Tensor index j takes row_counts[j] consecutive hidden units in order; they sum to 26624; offsets[j] differs from j * 3328 by at most 256; the largest count equals 3840.
All inputs are finite; a program needn't handle non-finite values.
Results may differ from a plain program's by a relative error of at most 0.0045.
Values may be sent and summed in bfloat16 or wider, within the bound.
No kernel may reach another device: no remote copies, remote signals or barrier semaphores. Data moves between devices by JAX's collectives and lax.ppermute only.
A program may use at most 192 MiB of HBM per device.

v0:
```python
import math
import jax
import jax.numpy as jnp
from jax import lax
from jax.sharding import PartitionSpec as P

DRIFT = 256
CAP = 3840
beta_first = 0.9
beta_second = 0.95
epsilon = 1e-08
decay_rate = 0.1
learn_rate = 0.001


def extended(cells, sides, width):
    for axis, dim in sides:
        count = lax.axis_size(axis)
        ends = count - 1
        head = lax.slice_in_dim(cells, 0, width, axis=dim)
        tail = lax.slice_in_dim(cells, cells.shape[dim] - width, cells.shape[dim], axis=dim)
        cells = jnp.concatenate(
            [
                lax.ppermute(tail, axis, [(i, (i + 1) % count) for i in range(ends)]),
                cells,
                lax.ppermute(head, axis, [((i + 1) % count, i) for i in range(ends)]),
            ],
            axis=dim,
        )
    return cells


def adamw(gradient, master, first_moment, second_moment, steps_done):
    first_new = beta_first * first_moment + (1.0 - beta_first) * gradient
    second_new = beta_second * second_moment + (1.0 - beta_second) * gradient * gradient
    first_fix = 1.0 - jnp.power(beta_first, steps_done)
    second_fix = 1.0 - jnp.power(beta_second, steps_done)
    update = (
        first_new / first_fix / (jnp.sqrt(second_new / second_fix) + epsilon) + decay_rate * master
    )
    master_new = master - learn_rate * update
    return (master_new, update)


def relayout(weights, row_counts):
    shard_rows = weights.shape[0]
    shard_width = weights.shape[1]
    offsets = jnp.cumsum(row_counts) - row_counts
    position = lax.axis_index("tensor")
    first_slot = lax.dynamic_index_in_dim(offsets, position, keepdims=False)
    length = lax.dynamic_index_in_dim(row_counts, position, keepdims=False)
    padded = extended(weights, (("tensor", 1),), DRIFT)
    widened = jnp.concatenate([padded, jnp.zeros((shard_rows, 2 * DRIFT), jnp.bfloat16)], axis=1)
    start = first_slot - position * shard_width + DRIFT
    window = lax.dynamic_slice_in_dim(widened, start, CAP, 1)
    slot_index = jnp.arange(CAP, dtype=jnp.int32)
    return jnp.where((slot_index < length)[None, :], window, jnp.zeros((), jnp.bfloat16))


def per_device(hidden, out_grad, master, first_moment, second_moment, row_counts, step_count):
    shard_rows = master.shape[0]
    hidden_units = hidden.shape[1]
    regrouped = lax.all_to_all(out_grad, "dp", split_axis=1, concat_axis=0, tiled=True)
    spread = lax.all_gather(regrouped, "tensor", axis=0, tiled=True)
    tensor_count = lax.axis_size("tensor")
    data_count = lax.axis_size("dp")
    local_tokens = out_grad.shape[0]
    group_tokens = hidden.shape[0]
    owned_cols = spread.reshape(tensor_count, data_count, local_tokens, shard_rows)
    shard_piece = lax.all_gather(hidden, "dp", axis=0, tiled=True)
    groups = shard_piece.shape[0] // group_tokens
    per_turn = math.gcd(groups, 4)
    turns = groups // per_turn
    activations = shard_piece.reshape(groups, tensor_count, local_tokens, hidden_units)

    def one_turn(turn_index, running):
        grad_block = lax.dynamic_slice_in_dim(owned_cols, turn_index * per_turn, per_turn, 1)
        act_block = lax.dynamic_slice_in_dim(activations, turn_index * per_turn, per_turn, 0)
        partial_value = jnp.einsum(
            "tgrd,gtrf->gdf", grad_block, act_block, preferred_element_type=jnp.float32
        )
        rounded = lax.optimization_barrier(partial_value.astype(jnp.bfloat16)).astype(jnp.float32)
        return running + jnp.sum(rounded, axis=0)

    gradient = lax.fori_loop(0, turns, one_turn, jnp.zeros((shard_rows, hidden_units), jnp.float32))
    steps_done = step_count[0].astype(jnp.float32)
    master_new, update = adamw(
        gradient,
        master,
        first_moment.astype(jnp.float32),
        second_moment.astype(jnp.float32),
        steps_done,
    )
    laid = relayout(master_new.astype(jnp.bfloat16), row_counts)
    outputs = [(update, laid)]
    joined = [jnp.concatenate([entry[slot] for entry in outputs], axis=0) for slot in range(2)]
    return (joined[0], joined[1])


def solution(mesh):
    return jax.shard_map(
        per_device,
        mesh=mesh,
        in_specs=(
            P("dp", "tensor"),
            P(("dp", "tensor"), None),
            P("dp", "tensor"),
            P("dp", "tensor"),
            P("dp", "tensor"),
            P(),
            P(),
        ),
        out_specs=(P("dp", "tensor"), P("dp", "tensor")),
        check_vma=False,
    )
```

profile of v0, /device:TPU:1, one launch (start us, length us, event | category | flops | bytes accessed | tf_op | source)
XLA Modules:
  0.0 353.1 jit_solution(3971043392902554566)
XLA Ops:
  7.2 0.0 all-gather.3.cloned.1.call-start
  7.2 1.0 copy.20
  8.2 23.1 %all_to_all.19 = bf16[16,32,256]{2,0,1:T(8,128)(2,1)} all-to-all(bf16[16,32,256]{2,0,1:T(8,128)(2,1)S(1)} %bitcast.22), channel_id=1, replica_groups=mesh['dp'=32,'tensor'=8] {'dp'}, dimensions={1} | all-to-all | bytes 524288 | tf_op jit(solution)/shard_map/all_to_all | solution.py:63
  31.3 0.0 all-gather.3.cloned.1.call-update
  31.3 0.0 all-gather.5.cloned.1.call-start
  31.4 0.7 all-gather.5.cloned.1.call-update
  32.8 0.8 reduce-window.9
  33.7 1.2 dynamic_slice.24
  34.9 0.7 bitcast_subtract_fusion
  35.6 21.4 %all-gather.3.cloned.1.call-done = bf16[4096,256]{1,0:T(8,128)(2,1)} async-done(((bf16[512,256]{1,0:T(8,128)(2,1)}), bf16[4096,256]{1,0:T(8,128)(2,1)}) %all-gather.3.cloned.1.call-update) | async-done | bytes 2097168 | tf_op jit(solution)/shard_map/all_gather | solution.py:64
  56.9 198.3 %all-gather.5.cloned.1.call-done = bf16[4096,3328]{1,0:T(8,128)(2,1)} async-done(((bf16[128,3328]{1,0:T(8,128)(2,1)}), bf16[4096,3328]{1,0:T(8,128)(2,1)}) %all-gather.5.cloned.1.call-update) | async-done | bytes 27262992 | tf_op jit(solution)/shard_map/all_gather | solution.py:70
  255.3 71.0 %while.14 = (s32[]{:T(128)}, f32[256,3328]{1,0:T(8,128)}, bf16[8,32,16,256]{3,2,1,0:T(8,128)(2,1)}, bf16[32,8,16,3328]{3,2,1,0:T(8,128)(2,1)}, s32[]{:T(128)}, /*index=5*/s32[]{:T(128)}, s32[]{:T(128)}, s32[]{:T(128)}) while((s32[]{:T(128)}, f32[256,3328]{1,0:T(8,128)}, bf16[8,32,16,256]{3,2,1,0:T(8,128)(2,1)}, ...), condition=%wide.region_2.0_spmd.clone, body=%wide.region_0.0_spmd.clone.sunk | while | flops 883490816 | bytes 30934164 | solution.py:85
  255.3 4.0 %bitcast_convert_fusion.2 = bf16[4,256,3328]{2,1,0:T(8,128)(2,1)S(1)} fusion(bf16[32,8,16,3328]{3,2,1,0:T(8,128)(2,1)} %get-tuple-element.165, s32[]{:T(128)S(6)} %select_n.26, bf16[8,32,16,256]{3,2,1,0:T(8,128)(2,1)} %get-tuple-element.164), kind=kOutput, calls=%fused_computation.clone.1 | convolution fusion | flops 875823104 | bytes 10486784 | tf_op jit(solution)/shard_map/while/body/eval_jaxpr/tgrd,gtrf->gdf/dot_general | solution.py:79
  259.3 1.0 convert_reduce_fusion.2
  260.3 2.1 select_add_fusion.2
  262.4 4.0 %bitcast_convert_fusion.2 = bf16[4,256,3328]{2,1,0:T(8,128)(2,1)S(1)} fusion(bf16[32,8,16,3328]{3,2,1,0:T(8,128)(2,1)} %get-tuple-element.165, s32[]{:T(128)S(6)} %select_n.26, bf16[8,32,16,256]{3,2,1,0:T(8,128)(2,1)} %get-tuple-element.164), kind=kOutput, calls=%fused_computation.clone.1 | convolution fusion | flops 875823104 | bytes 10486784 | tf_op jit(solution)/shard_map/while/body/eval_jaxpr/tgrd,gtrf->gdf/dot_general | solution.py:79
  266.4 1.0 convert_reduce_fusion.2
  267.4 4.1 %select_add_fusion.2 = f32[256,3328]{1,0:T(8,128)} fusion(f32[256,3328]{1,0:T(8,128)S(1)} %convert_reduce_fusion.2, f32[256,3328]{1,0:T(8,128)} %get-tuple-element.155, pred[]{:T(512)S(6)} %compare.3), kind=kLoop, calls=%fused_computation.2.clone.1 | loop fusion | flops 1703936 | bytes 10223617 | tf_op jit(solution)/shard_map/while/body/eval_jaxpr/add | solution.py:83
  271.5 4.0 %bitcast_convert_fusion.2 = bf16[4,256,3328]{2,1,0:T(8,128)(2,1)S(1)} fusion(bf16[32,8,16,3328]{3,2,1,0:T(8,128)(2,1)} %get-tuple-element.165, s32[]{:T(128)S(6)} %select_n.26, bf16[8,32,16,256]{3,2,1,0:T(8,128)(2,1)} %get-tuple-element.164), kind=kOutput, calls=%fused_computation.clone.1 | convolution fusion | flops 875823104 | bytes 10486784 | tf_op jit(solution)/shard_map/while/body/eval_jaxpr/tgrd,gtrf->gdf/dot_general | solution.py:79
  275.6 1.0 convert_reduce_fusion.2
  276.6 4.1 %select_add_fusion.2 = f32[256,3328]{1,0:T(8,128)} fusion(f32[256,3328]{1,0:T(8,128)S(1)} %convert_reduce_fusion.2, f32[256,3328]{1,0:T(8,128)} %get-tuple-element.155, pred[]{:T(512)S(6)} %compare.3), kind=kLoop, calls=%fused_computation.2.clone.1 | loop fusion | flops 1703936 | bytes 10223617 | tf_op jit(solution)/shard_map/while/body/eval_jaxpr/add | solution.py:83
  280.7 4.0 %bitcast_convert_fusion.2 = bf16[4,256,3328]{2,1,0:T(8,128)(2,1)S(1)} fusion(bf16[32,8,16,3328]{3,2,1,0:T(8,128)(2,1)} %get-tuple-element.165, s32[]{:T(128)S(6)} %select_n.26, bf16[8,32,16,256]{3,2,1,0:T(8,128)(2,1)} %get-tuple-element.164), kind=kOutput, calls=%fused_computation.clone.1 | convolution fusion | flops 875823104 | bytes 10486784 | tf_op jit(solution)/shard_map/while/body/eval_jaxpr/tgrd,gtrf->gdf/dot_general | solution.py:79
  284.7 1.0 convert_reduce_fusion.2
  285.7 4.1 %select_add_fusion.2 = f32[256,3328]{1,0:T(8,128)} fusion(f32[256,3328]{1,0:T(8,128)S(1)} %convert_reduce_fusion.2, f32[256,3328]{1,0:T(8,128)} %get-tuple-element.155, pred[]{:T(512)S(6)} %compare.3), kind=kLoop, calls=%fused_computation.2.clone.1 | loop fusion | flops 1703936 | bytes 10223617 | tf_op jit(solution)/shard_map/while/body/eval_jaxpr/add | solution.py:83
  289.8 4.0 %bitcast_convert_fusion.2 = bf16[4,256,3328]{2,1,0:T(8,128)(2,1)S(1)} fusion(bf16[32,8,16,3328]{3,2,1,0:T(8,128)(2,1)} %get-tuple-element.165, s32[]{:T(128)S(6)} %select_n.26, bf16[8,32,16,256]{3,2,1,0:T(8,128)(2,1)} %get-tuple-element.164), kind=kOutput, calls=%fused_computation.clone.1 | convolution fusion | flops 875823104 | bytes 10486784 | tf_op jit(solution)/shard_map/while/body/eval_jaxpr/tgrd,gtrf->gdf/dot_general | solution.py:79
  293.8 1.0 convert_reduce_fusion.2
  294.8 4.1 %select_add_fusion.2 = f32[256,3328]{1,0:T(8,128)} fusion(f32[256,3328]{1,0:T(8,128)S(1)} %convert_reduce_fusion.2, f32[256,3328]{1,0:T(8,128)} %get-tuple-element.155, pred[]{:T(512)S(6)} %compare.3), kind=kLoop, calls=%fused_computation.2.clone.1 | loop fusion | flops 1703936 | bytes 10223617 | tf_op jit(solution)/shard_map/while/body/eval_jaxpr/add | solution.py:83
  298.9 4.0 %bitcast_convert_fusion.2 = bf16[4,256,3328]{2,1,0:T(8,128)(2,1)S(1)} fusion(bf16[32,8,16,3328]{3,2,1,0:T(8,128)(2,1)} %get-tuple-element.165, s32[]{:T(128)S(6)} %select_n.26, bf16[8,32,16,256]{3,2,1,0:T(8,128)(2,1)} %get-tuple-element.164), kind=kOutput, calls=%fused_computation.clone.1 | convolution fusion | flops 875823104 | bytes 10486784 | tf_op jit(solution)/shard_map/while/body/eval_jaxpr/tgrd,gtrf->gdf/dot_general | solution.py:79
  302.9 1.0 convert_reduce_fusion.2
  303.9 4.1 %select_add_fusion.2 = f32[256,3328]{1,0:T(8,128)} fusion(f32[256,3328]{1,0:T(8,128)S(1)} %convert_reduce_fusion.2, f32[256,3328]{1,0:T(8,128)} %get-tuple-element.155, pred[]{:T(512)S(6)} %compare.3), kind=kLoop, calls=%fused_computation.2.clone.1 | loop fusion | flops 1703936 | bytes 10223617 | tf_op jit(solution)/shard_map/while/body/eval_jaxpr/add | solution.py:83
  308.0 4.0 %bitcast_convert_fusion.2 = bf16[4,256,3328]{2,1,0:T(8,128)(2,1)S(1)} fusion(bf16[32,8,16,3328]{3,2,1,0:T(8,128)(2,1)} %get-tuple-element.165, s32[]{:T(128)S(6)} %select_n.26, bf16[8,32,16,256]{3,2,1,0:T(8,128)(2,1)} %get-tuple-element.164), kind=kOutput, calls=%fused_computation.clone.1 | convolution fusion | flops 875823104 | bytes 10486784 | tf_op jit(solution)/shard_map/while/body/eval_jaxpr/tgrd,gtrf->gdf/dot_general | solution.py:79
  312.0 1.0 convert_reduce_fusion.2
  313.1 4.1 %select_add_fusion.2 = f32[256,3328]{1,0:T(8,128)} fusion(f32[256,3328]{1,0:T(8,128)S(1)} %convert_reduce_fusion.2, f32[256,3328]{1,0:T(8,128)} %get-tuple-element.155, pred[]{:T(512)S(6)} %compare.3), kind=kLoop, calls=%fused_computation.2.clone.1 | loop fusion | flops 1703936 | bytes 10223617 | tf_op jit(solution)/shard_map/while/body/eval_jaxpr/add | solution.py:83
  317.1 4.0 %bitcast_convert_fusion.2 = bf16[4,256,3328]{2,1,0:T(8,128)(2,1)S(1)} fusion(bf16[32,8,16,3328]{3,2,1,0:T(8,128)(2,1)} %get-tuple-element.165, s32[]{:T(128)S(6)} %select_n.26, bf16[8,32,16,256]{3,2,1,0:T(8,128)(2,1)} %get-tuple-element.164), kind=kOutput, calls=%fused_computation.clone.1 | convolution fusion | flops 875823104 | bytes 10486784 | tf_op jit(solution)/shard_map/while/body/eval_jaxpr/tgrd,gtrf->gdf/dot_general | solution.py:79
  321.2 1.0 convert_reduce_fusion.2
  322.2 4.1 %select_add_fusion.2 = f32[256,3328]{1,0:T(8,128)} fusion(f32[256,3328]{1,0:T(8,128)S(1)} %convert_reduce_fusion.2, f32[256,3328]{1,0:T(8,128)} %get-tuple-element.155, pred[]{:T(512)S(6)} %compare.3), kind=kLoop, calls=%fused_computation.2.clone.1 | loop fusion | flops 1703936 | bytes 10223617 | tf_op jit(solution)/shard_map/while/body/eval_jaxpr/add | solution.py:83
  326.3 6.5 %subtract_convert_fusion = (bf16[256,3328]{1,0:T(8,128)(2,1)S(1)}, f32[256,3328]{1,0:T(8,128)}) fusion(f32[256,3328]{1,0:T(8,128)} %param.11, f32[]{:T(128)} %bitcast.5, f32[256,3328]{1,0:T(8,128)} %get-tuple-element.81, bf16[256,3328]{1,0:T(8,128)(2,1)} %param.13, f32[]{:T(128)} %bitcast.4, bf16[256,3328]{1,0:T(8,128)(2,1)} %param.12), kind=kLoop, calls=%fused_computation.14 | loop fusion | flops 15335424 | bytes 15335432 | tf_op jit(solution)/shard_map/convert_element_type | solution.py:94
  332.8 4.0 %collective-permute-start = (bf16[256,256]{1,0:T(8,128)(2,1)S(1)}, bf16[256,256]{1,0:T(8,128)(2,1)S(1)}, u32[]{:S(2)}, u32[]{:S(2)}) collective-permute-start(bf16[256,256]{1,0:T(8,128)(2,1)S(1)} %get-tuple-element.120), channel_id=1, source_target_pairs={{0,1},{1,2},{2,3},{3,4},{4,5},{5,6},{6,7},{8,9},{9,10},{10,11},{11... | collective-permute-start | bytes 393224 | tf_op jit(solution)/shard_map/ppermute | solution.py:24
  336.8 1.9 collective-permute-start.1
  338.7 0.6 iota_compare_fusion
  339.4 0.6 dynamic_slice.25
  340.6 0.1 pad_dynamic-slice_fusion.3
  340.7 0.0 collective-permute-done
  340.7 2.4 collective-permute-done.1
  343.1 3.1 fusion.12
  (3 shorter events, 0.0 us)
Async XLA Ops:
  7.2 49.8 %all-gather.3.cloned.1.call-start = ((), (), s32[]{:S(2)}) async-start(), calls=%async_computation.1 | async-start | bytes 2359296 | tf_op jit(solution)/shard_map/all_gather | solution.py:64
  31.3 223.9 %all-gather.5.cloned.1.call-start = ((), (), s32[]{:S(2)}) async-start(), calls=%async_computation.2 | async-start | bytes 28114944 | tf_op jit(solution)/shard_map/all_gather | solution.py:70
  332.8 7.9 %collective-permute-start = (bf16[256,256]{1,0:T(8,128)(2,1)S(1)}, bf16[256,256]{1,0:T(8,128)(2,1)S(1)}, u32[]{:S(2)}, u32[]{:S(2)}) collective-permute-start(bf16[256,256]{1,0:T(8,128)(2,1)S(1)} %get-tuple-element.120), channel_id=1, source_target_pairs={{0,1},{1,2},{2,3},{3,4},{4,5},{5,6},{6,7},{8,9},{9,10},{10,11},{11... | collective-permute-start | bytes 393224 | tf_op jit(solution)/shard_map/ppermute | solution.py:24
  336.8 6.3 %collective-permute-start.1 = (bf16[256,256]{1,0:T(8,128)(2,1)S(1)}, bf16[256,256]{1,0:T(8,128)(2,1)S(1)}, u32[]{:S(2)}, u32[]{:S(2)}) collective-permute-start(bf16[256,256]{1,0:T(8,128)(2,1)S(1)} %get-tuple-element.119), channel_id=1, source_target_pairs={{1,0},{2,1},{3,2},{4,3},{5,4},{6,5},{7,6},{9,8},{10,9},{11,10},{12... | collective-permute-start | bytes 393224 | tf_op jit(solution)/shard_map/ppermute | solution.py:26
Sparse Core Ops, SparseCore 0:
  31.5 25.4 all-gather.2
  59.5 195.6 all-gather.4
where the time goes:
time: 354 us; the launch traced here: 353 us
  waiting for transfers between devices  223 us (63%)
  other arithmetic  50.5 us (14%)
  matrix products  32.1 us (9%)
  blocking collectives  23.1 us (7%)
  between operations  15.5 us (4%)
  starting transfers between devices  6.03 us (2%)
    all_gather x1, waiting for transfers between devices, per_device(): shard_piece = lax.all_gather(hidden, 'dp', axis=0, tiled=True)  198 us
    dot_general x8, matrix products, one_turn(): jnp.einsum('tgrd,gtrf->gdf', grad_block, act_block, preferred_element_typ...  32.1 us
    add x8, other arithmetic, one_turn(): return running + jnp.sum(rounded, axis=0)  30.8 us
    all_to_all x1, blocking collectives, per_device(): lax.all_to_all(out_grad, 'dp', split_axis=1, concat_axis=0, tiled=True)  23.1 us
    all_gather x1, waiting for transfers between devices, per_device(): spread = lax.all_gather(regrouped, 'tensor', axis=0, tiled=True)  21.4 us
    reduce_sum x8, other arithmetic, one_turn(): return running + jnp.sum(rounded, axis=0)  7.96 us
  transfers between devices with their start and end apart: 4, of which 3 were waited for; matrix products, arithmetic and copies ran while one was open for 1% of the time, Pallas kernels for 0%

commit v1 on v0

--- a/solution.py
+++ b/solution.py
@@ -11,6 +11,14 @@
 epsilon = 1e-08
 decay_rate = 0.1
 learn_rate = 0.001
+
+
+def manage_frame(work_x, where_dim):
+    work_x = jnp.moveaxis(work_x, 0, where_dim)
+    w_next = work_x.shape
+    return work_x.reshape(
+        *w_next[:where_dim], w_next[where_dim] * w_next[where_dim + 1], *w_next[where_dim + 2 :]
+    )
 
 
 def extended(cells, sides, width):
@@ -61,7 +69,23 @@
     shard_rows = master.shape[0]
     hidden_units = hidden.shape[1]
     regrouped = lax.all_to_all(out_grad, "dp", split_axis=1, concat_axis=0, tiled=True)
-    spread = lax.all_gather(regrouped, "tensor", axis=0, tiled=True)
+    q_n = lax.axis_size("tensor")
+    views = tuple(((dd, (dd + 1) % q_n) for dd in range(q_n)))
+    rows = tuple(((src_i, to_i) for to_i, src_i in views))
+    local_next, inter = ([], [])
+    nth = 0
+    while nth < q_n - 1:
+        if nth % 2 == 0:
+            local_next.append(
+                lax.ppermute(local_next[-1] if local_next else regrouped, "tensor", views)
+            )
+        else:
+            inter.append(lax.ppermute(inter[-1] if inter else regrouped, "tensor", rows))
+        nth += 1
+    local_part = jnp.stack([*local_next[::-1], regrouped, *inter], axis=0)
+    x_new = lax.axis_index("tensor") - len(local_next)
+    local_part = local_part[(jnp.arange(q_n) - x_new) % q_n]
+    spread = manage_frame(local_part, 0)
     tensor_count = lax.axis_size("tensor")
     data_count = lax.axis_size("dp")
     local_tokens = out_grad.shape[0]

time: 354 us -> 309 us (0.87)
  waiting for transfers between devices: 223 us -> 159 us
  starting transfers between devices: 6.03 us -> 20.7 us
  local copies, waits for them, and re-layouts: 2.92 us -> 7.01 us
    all_gather x1, waiting for transfers between devices: 198 us -> 145 us  [per_device(): shard_piece = lax.all_gather(hidden, 'dp', axis=0, tiled=True)]
    all_gather x1 -> x0, waiting for transfers between devices: 21.4 us -> none  [per_device(): spread = lax.all_gather(regrouped, 'tensor', axis=0, tiled=True)]
    ppermute x0 -> x7, starting transfers between devices: none -> 14.7 us  [the longest x4 11.1 us: per_device(): lax.ppermute(local_next[-1] if local_next else regrouped, 'tensor', views)]
    ppermute x0 -> x7, waiting for transfers between devices: none -> 10.6 us  [the longest x4 8.47 us: per_device(): lax.ppermute(local_next[-1] if local_next else regrouped, 'tensor', views)]
  transfers between devices with their start and end apart: 4 -> 10, of which waited for: 3 -> 7; matrix products, arithmetic and copies ran while one was open for 1% -> 3% of each run, Pallas kernels for 0% -> 0%
where the time goes in v1:
time: 309 us; the launch traced here: 308 us
  waiting for transfers between devices  159 us (51%)
  other arithmetic  50.5 us (16%)
  matrix products  32.1 us (10%)
  blocking collectives  23 us (7%)
  starting transfers between devices  20.7 us (7%)
  between operations  15.5 us (5%)
  local copies, waits for them, and re-layouts  7.01 us (2%)
    all_gather x1, waiting for transfers between devices, per_device(): shard_piece = lax.all_gather(hidden, 'dp', axis=0, tiled=True)  145 us
    dot_general x8, matrix products, one_turn(): jnp.einsum('tgrd,gtrf->gdf', grad_block, act_block, preferred_element_typ...  32.1 us
    add x8, other arithmetic, one_turn(): return running + jnp.sum(rounded, axis=0)  30.8 us
    all_to_all x1, blocking collectives, per_device(): lax.all_to_all(out_grad, 'dp', split_axis=1, concat_axis=0, tiled=True)  23 us
    ppermute x4, starting transfers between devices, per_device(): lax.ppermute(local_next[-1] if local_next else regrouped, 'tensor', views)  11.1 us
    ppermute x4, waiting for transfers between devices, per_device(): lax.ppermute(local_next[-1] if local_next else regrouped, 'tensor', views)  8.47 us
    reduce_sum x8, other arithmetic, one_turn(): return running + jnp.sum(rounded, axis=0)  7.96 us
    convert_element_type x1, other arithmetic, per_device(): laid = relayout(master_new.astype(jnp.bfloat16), row_counts)  6.5 us
  transfers between devices with their start and end apart: 10, of which 7 were waited for; matrix products, arithmetic and copies ran while one was open for 3% of the time, Pallas kernels for 0%

profile of v1, /device:TPU:1, one launch (start us, length us, event | category | flops | bytes accessed | tf_op | source)
XLA Modules:
  0.0 308.0 jit_solution(16727883591767059211)
XLA Ops:
  7.9 1.0 copy.21
  8.9 23.0 %all_to_all.19 = bf16[16,32,256]{2,0,1:T(8,128)(2,1)S(1)} all-to-all(bf16[16,32,256]{2,0,1:T(8,128)(2,1)S(1)} %bitcast.43), channel_id=1, replica_groups=mesh['dp'=32,'tensor'=8] {'dp'}, dimensions={1} | all-to-all | bytes 524288 | tf_op jit(solution)/shard_map/all_to_all | solution.py:71
  31.9 3.7 %collective-permute-start = (bf16[512,256]{1,0:T(8,128)(2,1)S(1)}, bf16[512,256]{1,0:T(8,128)(2,1)S(1)}, u32[]{:S(2)}, u32[]{:S(2)}) collective-permute-start(bf16[512,256]{1,0:T(8,128)(2,1)S(1)} %bitcast.40), channel_id=1, source_target_pairs={{0,1},{1,2},{2,3},{3,4},{4,5},{5,6},{6,7},{7,0},{8,9},{9,10},{10,1... | collective-permute-start | bytes 786440 | tf_op jit(solution)/shard_map/ppermute | solution.py:80
  35.5 3.3 %collective-permute-done = bf16[512,256]{1,0:T(8,128)(2,1)S(1)} collective-permute-done((bf16[512,256]{1,0:T(8,128)(2,1)S(1)}, bf16[512,256]{1,0:T(8,128)(2,1)S(1)}, u32[]{:S(2)}, u32[]{:S(2)}) %collective-permute-start) | collective-permute-done | bytes 262176 | tf_op jit(solution)/shard_map/ppermute | solution.py:80
  38.9 2.5 collective-permute-start.1
  41.5 3.2 %collective-permute-done.1 = bf16[512,256]{1,0:T(8,128)(2,1)S(1)} collective-permute-done((bf16[512,256]{1,0:T(8,128)(2,1)S(1)}, bf16[512,256]{1,0:T(8,128)(2,1)S(1)}, u32[]{:S(2)}, u32[]{:S(2)}) %collective-permute-start.1) | collective-permute-done | bytes 262176 | tf_op jit(solution)/shard_map/ppermute | solution.py:80
  44.7 2.5 collective-permute-start.2
  47.5 1.0 collective-permute-start.5
  48.5 2.0 collective-permute-done.2
  50.5 2.5 collective-permute-start.3
  53.7 0.8 reduce-window.9
  54.5 1.3 dynamic_slice.24
  56.4 2.5 collective-permute-start.6
  59.0 1.0 bitcast_dynamic-update-slice_fusion.6
  60.1 1.0 bitcast_dynamic-update-slice_fusion.1
  61.1 1.8 collective-permute-done.6
  62.9 2.0 gather_fusion
  64.9 145.3 %all-gather.2.cloned.1.call-done = bf16[4096,3328]{1,0:T(8,128)(2,1)} async-done(((bf16[128,3328]{1,0:T(8,128)(2,1)}), bf16[4096,3328]{1,0:T(8,128)(2,1)}) %all-gather.2.cloned.1.call-update) | async-done | bytes 27262992 | tf_op jit(solution)/shard_map/all_gather | solution.py:94
  210.2 71.0 %while.14 = (s32[]{:T(128)}, f32[256,3328]{1,0:T(8,128)}, bf16[8,32,16,256]{3,2,1,0:T(8,128)(2,1)}, bf16[32,8,16,3328]{3,2,1,0:T(8,128)(2,1)}, s32[]{:T(128)}, /*index=5*/s32[]{:T(128)}, s32[]{:T(128)}, s32[]{:T(128)}) while((s32[]{:T(128)}, f32[256,3328]{1,0:T(8,128)}, bf16[8,32,16,256]{3,2,1,0:T(8,128)(2,1)}, ...), condition=%wide.region_2.3_spmd.clone, body=%wide.region_0.2_spmd.clone.sunk | while | flops 883490816 | bytes 30934164 | solution.py:109
  210.2 4.0 %bitcast_convert_fusion.2 = bf16[4,256,3328]{2,1,0:T(8,128)(2,1)S(1)} fusion(bf16[32,8,16,3328]{3,2,1,0:T(8,128)(2,1)} %get-tuple-element.165, s32[]{:T(128)S(6)} %select_n.60, bf16[8,32,16,256]{3,2,1,0:T(8,128)(2,1)} %get-tuple-element.164), kind=kOutput, calls=%fused_computation.1.clone.1 | convolution fusion | flops 875823104 | bytes 10486784 | tf_op jit(solution)/shard_map/while/body/eval_jaxpr/tgrd,gtrf->gdf/dot_general | solution.py:103
  214.2 1.0 convert_reduce_fusion.2
  215.2 2.1 select_add_fusion.2
  217.3 4.0 %bitcast_convert_fusion.2 = bf16[4,256,3328]{2,1,0:T(8,128)(2,1)S(1)} fusion(bf16[32,8,16,3328]{3,2,1,0:T(8,128)(2,1)} %get-tuple-element.165, s32[]{:T(128)S(6)} %select_n.60, bf16[8,32,16,256]{3,2,1,0:T(8,128)(2,1)} %get-tuple-element.164), kind=kOutput, calls=%fused_computation.1.clone.1 | convolution fusion | flops 875823104 | bytes 10486784 | tf_op jit(solution)/shard_map/while/body/eval_jaxpr/tgrd,gtrf->gdf/dot_general | solution.py:103
  221.4 1.0 convert_reduce_fusion.2
  222.4 4.1 %select_add_fusion.2 = f32[256,3328]{1,0:T(8,128)} fusion(f32[256,3328]{1,0:T(8,128)S(1)} %convert_reduce_fusion.2, f32[256,3328]{1,0:T(8,128)} %get-tuple-element.155, pred[]{:T(512)S(6)} %compare.10), kind=kLoop, calls=%fused_computation.3.clone.1 | loop fusion | flops 1703936 | bytes 10223617 | tf_op jit(solution)/shard_map/while/body/eval_jaxpr/add | solution.py:107
  226.5 4.0 %bitcast_convert_fusion.2 = bf16[4,256,3328]{2,1,0:T(8,128)(2,1)S(1)} fusion(bf16[32,8,16,3328]{3,2,1,0:T(8,128)(2,1)} %get-tuple-element.165, s32[]{:T(128)S(6)} %select_n.60, bf16[8,32,16,256]{3,2,1,0:T(8,128)(2,1)} %get-tuple-element.164), kind=kOutput, calls=%fused_computation.1.clone.1 | convolution fusion | flops 875823104 | bytes 10486784 | tf_op jit(solution)/shard_map/while/body/eval_jaxpr/tgrd,gtrf->gdf/dot_general | solution.py:103
  230.5 1.0 convert_reduce_fusion.2
  231.5 4.1 %select_add_fusion.2 = f32[256,3328]{1,0:T(8,128)} fusion(f32[256,3328]{1,0:T(8,128)S(1)} %convert_reduce_fusion.2, f32[256,3328]{1,0:T(8,128)} %get-tuple-element.155, pred[]{:T(512)S(6)} %compare.10), kind=kLoop, calls=%fused_computation.3.clone.1 | loop fusion | flops 1703936 | bytes 10223617 | tf_op jit(solution)/shard_map/while/body/eval_jaxpr/add | solution.py:107
  235.6 4.0 %bitcast_convert_fusion.2 = bf16[4,256,3328]{2,1,0:T(8,128)(2,1)S(1)} fusion(bf16[32,8,16,3328]{3,2,1,0:T(8,128)(2,1)} %get-tuple-element.165, s32[]{:T(128)S(6)} %select_n.60, bf16[8,32,16,256]{3,2,1,0:T(8,128)(2,1)} %get-tuple-element.164), kind=kOutput, calls=%fused_computation.1.clone.1 | convolution fusion | flops 875823104 | bytes 10486784 | tf_op jit(solution)/shard_map/while/body/eval_jaxpr/tgrd,gtrf->gdf/dot_general | solution.py:103
  239.6 1.0 convert_reduce_fusion.2
  240.6 4.1 %select_add_fusion.2 = f32[256,3328]{1,0:T(8,128)} fusion(f32[256,3328]{1,0:T(8,128)S(1)} %convert_reduce_fusion.2, f32[256,3328]{1,0:T(8,128)} %get-tuple-element.155, pred[]{:T(512)S(6)} %compare.10), kind=kLoop, calls=%fused_computation.3.clone.1 | loop fusion | flops 1703936 | bytes 10223617 | tf_op jit(solution)/shard_map/while/body/eval_jaxpr/add | solution.py:107
  244.7 4.0 %bitcast_convert_fusion.2 = bf16[4,256,3328]{2,1,0:T(8,128)(2,1)S(1)} fusion(bf16[32,8,16,3328]{3,2,1,0:T(8,128)(2,1)} %get-tuple-element.165, s32[]{:T(128)S(6)} %select_n.60, bf16[8,32,16,256]{3,2,1,0:T(8,128)(2,1)} %get-tuple-element.164), kind=kOutput, calls=%fused_computation.1.clone.1 | convolution fusion | flops 875823104 | bytes 10486784 | tf_op jit(solution)/shard_map/while/body/eval_jaxpr/tgrd,gtrf->gdf/dot_general | solution.py:103
  248.7 1.0 convert_reduce_fusion.2
  249.7 4.1 %select_add_fusion.2 = f32[256,3328]{1,0:T(8,128)} fusion(f32[256,3328]{1,0:T(8,128)S(1)} %convert_reduce_fusion.2, f32[256,3328]{1,0:T(8,128)} %get-tuple-element.155, pred[]{:T(512)S(6)} %compare.10), kind=kLoop, calls=%fused_computation.3.clone.1 | loop fusion | flops 1703936 | bytes 10223617 | tf_op jit(solution)/shard_map/while/body/eval_jaxpr/add | solution.py:107
  253.8 4.0 %bitcast_convert_fusion.2 = bf16[4,256,3328]{2,1,0:T(8,128)(2,1)S(1)} fusion(bf16[32,8,16,3328]{3,2,1,0:T(8,128)(2,1)} %get-tuple-element.165, s32[]{:T(128)S(6)} %select_n.60, bf16[8,32,16,256]{3,2,1,0:T(8,128)(2,1)} %get-tuple-element.164), kind=kOutput, calls=%fused_computation.1.clone.1 | convolution fusion | flops 875823104 | bytes 10486784 | tf_op jit(solution)/shard_map/while/body/eval_jaxpr/tgrd,gtrf->gdf/dot_general | solution.py:103
  257.9 1.0 convert_reduce_fusion.2
  258.9 4.1 %select_add_fusion.2 = f32[256,3328]{1,0:T(8,128)} fusion(f32[256,3328]{1,0:T(8,128)S(1)} %convert_reduce_fusion.2, f32[256,3328]{1,0:T(8,128)} %get-tuple-element.155, pred[]{:T(512)S(6)} %compare.10), kind=kLoop, calls=%fused_computation.3.clone.1 | loop fusion | flops 1703936 | bytes 10223617 | tf_op jit(solution)/shard_map/while/body/eval_jaxpr/add | solution.py:107
  263.0 4.0 %bitcast_convert_fusion.2 = bf16[4,256,3328]{2,1,0:T(8,128)(2,1)S(1)} fusion(bf16[32,8,16,3328]{3,2,1,0:T(8,128)(2,1)} %get-tuple-element.165, s32[]{:T(128)S(6)} %select_n.60, bf16[8,32,16,256]{3,2,1,0:T(8,128)(2,1)} %get-tuple-element.164), kind=kOutput, calls=%fused_computation.1.clone.1 | convolution fusion | flops 875823104 | bytes 10486784 | tf_op jit(solution)/shard_map/while/body/eval_jaxpr/tgrd,gtrf->gdf/dot_general | solution.py:103
  267.0 1.0 convert_reduce_fusion.2
  268.0 4.1 %select_add_fusion.2 = f32[256,3328]{1,0:T(8,128)} fusion(f32[256,3328]{1,0:T(8,128)S(1)} %convert_reduce_fusion.2, f32[256,3328]{1,0:T(8,128)} %get-tuple-element.155, pred[]{:T(512)S(6)} %compare.10), kind=kLoop, calls=%fused_computation.3.clone.1 | loop fusion | flops 1703936 | bytes 10223617 | tf_op jit(solution)/shard_map/while/body/eval_jaxpr/add | solution.py:107
  272.1 4.0 %bitcast_convert_fusion.2 = bf16[4,256,3328]{2,1,0:T(8,128)(2,1)S(1)} fusion(bf16[32,8,16,3328]{3,2,1,0:T(8,128)(2,1)} %get-tuple-element.165, s32[]{:T(128)S(6)} %select_n.60, bf16[8,32,16,256]{3,2,1,0:T(8,128)(2,1)} %get-tuple-element.164), kind=kOutput, calls=%fused_computation.1.clone.1 | convolution fusion | flops 875823104 | bytes 10486784 | tf_op jit(solution)/shard_map/while/body/eval_jaxpr/tgrd,gtrf->gdf/dot_general | solution.py:103
  276.1 1.0 convert_reduce_fusion.2
  277.1 4.1 %select_add_fusion.2 = f32[256,3328]{1,0:T(8,128)} fusion(f32[256,3328]{1,0:T(8,128)S(1)} %convert_reduce_fusion.2, f32[256,3328]{1,0:T(8,128)} %get-tuple-element.155, pred[]{:T(512)S(6)} %compare.10), kind=kLoop, calls=%fused_computation.3.clone.1 | loop fusion | flops 1703936 | bytes 10223617 | tf_op jit(solution)/shard_map/while/body/eval_jaxpr/add | solution.py:107
  281.2 6.5 %subtract_convert_fusion = (bf16[256,3328]{1,0:T(8,128)(2,1)S(1)}, f32[256,3328]{1,0:T(8,128)}) fusion(f32[256,3328]{1,0:T(8,128)} %param.11, f32[]{:T(128)} %bitcast.15, f32[256,3328]{1,0:T(8,128)} %get-tuple-element.81, bf16[256,3328]{1,0:T(8,128)(2,1)} %param.13, f32[]{:T(128)} %bitcast.14, bf16[256,3328]{1,0:T(8,128)(2,1)} %param.12), kind=kLoop, calls=%fused_computation.15 | loop fusion | flops 15335424 | bytes 15335432 | tf_op jit(solution)/shard_map/convert_element_type | solution.py:118
  287.7 4.0 %collective-permute-start.7 = (bf16[256,256]{1,0:T(8,128)(2,1)S(1)}, bf16[256,256]{1,0:T(8,128)(2,1)S(1)}, u32[]{:S(2)}, u32[]{:S(2)}) collective-permute-start(bf16[256,256]{1,0:T(8,128)(2,1)S(1)} %get-tuple-element.120), channel_id=1, source_target_pairs={{0,1},{1,2},{2,3},{3,4},{4,5},{5,6},{6,7},{8,9},{9,10},{10,11},{11... | collective-permute-start | bytes 393224 | tf_op jit(solution)/shard_map/ppermute | solution.py:32
  291.8 1.9 collective-permute-start.8
  295.7 2.4 collective-permute-done.8
  298.0 3.1 %fusion.12 = bf16[256,3840]{1,0:T(8,128)(2,1)} fusion(s32[]{:T(128)S(6)} %select_n.47, bf16[256,256]{1,0:T(8,128)(2,1)S(1)} %collective-permute-done.7, bf16[256,3328]{1,0:T(8,128)(2,1)S(1)} %get-tuple-element.117, bf16[256,256]{1,0:T(8,128)(2,1)S(1)} %collective-permute-done.8, pred[3840]{0:T(1024)(128)(4,1)S(1)} %iota_compare_fusion, ...), kind=kLoop, calls=%fused_computation.23 | loop fusion | flops 8847360 | bytes 3943684 | tf_op jit(solution)/shard_map/jit(_where)/select_n | solution.py:65
  (22 shorter events, 3.4 us)
Async XLA Ops:
  7.2 203.0 %all-gather.2.cloned.1.call-start = ((), (), s32[]{:S(2)}) async-start(), calls=%async_computation.1 | async-start | bytes 28114944 | tf_op jit(solution)/shard_map/all_gather | solution.py:94
  31.9 7.0 %collective-permute-start = (bf16[512,256]{1,0:T(8,128)(2,1)S(1)}, bf16[512,256]{1,0:T(8,128)(2,1)S(1)}, u32[]{:S(2)}, u32[]{:S(2)}) collective-permute-start(bf16[512,256]{1,0:T(8,128)(2,1)S(1)} %bitcast.40), channel_id=1, source_target_pairs={{0,1},{1,2},{2,3},{3,4},{4,5},{5,6},{6,7},{7,0},{8,9},{9,10},{10,1... | collective-permute-start | bytes 786440 | tf_op jit(solution)/shard_map/ppermute | solution.py:80
  38.9 5.8 %collective-permute-start.1 = (bf16[512,256]{1,0:T(8,128)(2,1)S(1)}, bf16[512,256]{1,0:T(8,128)(2,1)S(1)}, u32[]{:S(2)}, u32[]{:S(2)}) collective-permute-start(bf16[512,256]{1,0:T(8,128)(2,1)S(1)} %collective-permute-done), channel_id=1, source_target_pairs={{0,1},{1,2},{2,3},{3,4},{4,5},{5,6},{6,7},{7,0},{8,9},{9,10},{10,1... | collective-permute-start | bytes 786440 | tf_op jit(solution)/shard_map/ppermute | solution.py:80
  41.3 6.2 %collective-permute-start.4 = (bf16[512,256]{1,0:T(8,128)(2,1)S(1)}, bf16[512,256]{1,0:T(8,128)(2,1)S(1)}, u32[]{:S(2)}, u32[]{:S(2)}) collective-permute-start(bf16[512,256]{1,0:T(8,128)(2,1)S(1)} %bitcast.41), channel_id=1, source_target_pairs={{1,0},{2,1},{3,2},{4,3},{5,4},{6,5},{7,6},{0,7},{9,8},{10,9},{11,1... | collective-permute-start | bytes 786440 | tf_op jit(solution)/shard_map/ppermute | solution.py:83
  44.7 5.8 %collective-permute-start.2 = (bf16[512,256]{1,0:T(8,128)(2,1)S(1)}, bf16[512,256]{1,0:T(8,128)(2,1)S(1)}, u32[]{:S(2)}, u32[]{:S(2)}) collective-permute-start(bf16[512,256]{1,0:T(8,128)(2,1)S(1)} %collective-permute-done.1), channel_id=1, source_target_pairs={{0,1},{1,2},{2,3},{3,4},{4,5},{5,6},{6,7},{7,0},{8,9},{9,10},{10,1... | collective-permute-start | bytes 786440 | tf_op jit(solution)/shard_map/ppermute | solution.py:80
  47.5 8.9 %collective-permute-start.5 = (bf16[512,256]{1,0:T(8,128)(2,1)S(1)}, bf16[512,256]{1,0:T(8,128)(2,1)}, u32[]{:S(2)}, u32[]{:S(2)}) collective-permute-start(bf16[512,256]{1,0:T(8,128)(2,1)S(1)} %collective-permute-done.4), channel_id=1, source_target_pairs={{1,0},{2,1},{3,2},{4,3},{5,4},{6,5},{7,6},{0,7},{9,8},{10,9},{11,1... | collective-permute-start | bytes 786440 | tf_op jit(solution)/shard_map/ppermute | solution.py:83
  50.5 8.5 %collective-permute-start.3 = (bf16[512,256]{1,0:T(8,128)(2,1)S(1)}, bf16[512,256]{1,0:T(8,128)(2,1)}, u32[]{:S(2)}, u32[]{:S(2)}) collective-permute-start(bf16[512,256]{1,0:T(8,128)(2,1)S(1)} %collective-permute-done.2), channel_id=1, source_target_pairs={{0,1},{1,2},{2,3},{3,4},{4,5},{5,6},{6,7},{7,0},{8,9},{9,10},{10,1... | collective-permute-start | bytes 786440 | tf_op jit(solution)/shard_map/ppermute | solution.py:80
  56.4 6.4 %collective-permute-start.6 = (bf16[512,256]{1,0:T(8,128)(2,1)}, bf16[512,256]{1,0:T(8,128)(2,1)S(1)}, u32[]{:S(2)}, u32[]{:S(2)}) collective-permute-start(bf16[512,256]{1,0:T(8,128)(2,1)} %collective-permute-done.5), channel_id=1, source_target_pairs={{1,0},{2,1},{3,2},{4,3},{5,4},{6,5},{7,6},{0,7},{9,8},{10,9},{11,1... | collective-permute-start | bytes 786440 | tf_op jit(solution)/shard_map/ppermute | solution.py:83
  287.7 8.0 %collective-permute-start.7 = (bf16[256,256]{1,0:T(8,128)(2,1)S(1)}, bf16[256,256]{1,0:T(8,128)(2,1)S(1)}, u32[]{:S(2)}, u32[]{:S(2)}) collective-permute-start(bf16[256,256]{1,0:T(8,128)(2,1)S(1)} %get-tuple-element.120), channel_id=1, source_target_pairs={{0,1},{1,2},{2,3},{3,4},{4,5},{5,6},{6,7},{8,9},{9,10},{10,11},{11... | collective-permute-start | bytes 393224 | tf_op jit(solution)/shard_map/ppermute | solution.py:32
  291.8 6.3 %collective-permute-start.8 = (bf16[256,256]{1,0:T(8,128)(2,1)S(1)}, bf16[256,256]{1,0:T(8,128)(2,1)S(1)}, u32[]{:S(2)}, u32[]{:S(2)}) collective-permute-start(bf16[256,256]{1,0:T(8,128)(2,1)S(1)} %get-tuple-element.119), channel_id=1, source_target_pairs={{1,0},{2,1},{3,2},{4,3},{5,4},{6,5},{7,6},{9,8},{10,9},{11,10},{12... | collective-permute-start | bytes 393224 | tf_op jit(solution)/shard_map/ppermute | solution.py:34
Sparse Core Ops, SparseCore 0:
  10.6 199.5 all-gather.1
